TPU v7x, 32 devices: a whole 2x2x4 slice. The times are simulated.
32 devices in a mesh: dom: 16 (over z, y, x), chan: 2 (over core).
Axes of the slice: x: 2, y: 2, z: 4, core: 2. Of those that a mesh axis runs over, the one named last changes fastest.
Arguments:
- features: bfloat16 [16384, 512], P('dom', 'chan'), may hold values from -6 to 6
- w_self: bfloat16 [512, 512], P('chan'), may hold values from -0.25 to 0.25
- w_neigh: bfloat16 [512, 512], P('chan'), may hold values from -1.5 to 1.5
- degrees: int32 [16384], P('dom'), may hold values from 16 to 48
- local_src: int32 [128], P('dom'), may hold values from 0 to 7
- local_dst: int32 [128], P('dom'), may hold values from 0 to 7
- local_tiles: bfloat16 [128, 128, 128], P('dom'), may hold values from 0 to 1, as said below
- remote_src: int32 [256], P('dom'), may hold values from 0 to 7
- remote_part: int32 [256, 1], P('dom'), may hold values from 0 to 15; in each aligned block of 16 rows (0 to 15, 16 to 31, ...) at most 2 rows name the same one
- remote_dst: int32 [256], P('dom'), may hold values from 0 to 7
- remote_tiles: bfloat16 [256, 128, 128], P('dom'), may hold values from 0 to 1, as said below
- cotangent: bfloat16 [16384, 512], P('dom', 'chan'), may hold values from -6 to 6
Outputs:
- output: bfloat16 [16384, 512], P('dom', 'chan')
- grad_self: float32 [512, 512], P('chan')
- grad_neigh: float32 [512, 512], P('chan')
- grad_features: bfloat16 [16384, 512], P('dom', 'chan')
Inputs may be any that keep to these rules, and one draw needn't show every extreme that they name: `remote_part`: among the 16 remote tiles of one partition each partition is named at most 2 times, a bound that some block reaches. `local_tiles`: every entry is 0 or 1. `remote_tiles`: every entry is 0 or 1.
All inputs are finite; a program needn't handle non-finite values.
Results may differ from a plain program's by a relative error of at most 0.015.
Values may be sent and summed in bfloat16 or wider, within the bound.
No kernel may reach another device: no remote copies, remote signals or barrier semaphores. Data moves between devices by JAX's collectives and lax.ppermute only.
A program may use at most 64 MiB of HBM per device.

v0:
```python
import math
import jax
import jax.numpy as jnp
from jax import lax
from jax.sharding import PartitionSpec as P

TILE = 128
CAP = 2


def silu_slope(value):
    sig = jax.nn.sigmoid(value)
    return sig * (1.0 + value * (1.0 - sig))


def tile_products(tiles, sources, feat_blocks):
    picked = jnp.take(feat_blocks, sources, axis=0)
    return jnp.einsum("tij,tic->tjc", tiles, picked, preferred_element_type=jnp.float32)


def local_sum(local_tiles, local_src, local_dst, feat_blocks, block_count):
    terms = tile_products(local_tiles, local_src, feat_blocks)
    onehot = (jnp.arange(block_count, dtype=jnp.int32)[:, None] == local_dst[None, :]).astype(
        jnp.float32
    )
    flat = terms.reshape(terms.shape[0], -1)
    return jnp.einsum("bt,tk->bk", onehot, flat, precision=lax.Precision.HIGHEST)


def push_partials(outgoing, out_blocks):
    return (
        lax.all_to_all(outgoing, "dom", split_axis=0, concat_axis=0, tiled=True),
        lax.all_to_all(out_blocks, "dom", split_axis=0, concat_axis=0, tiled=True),
    )


def per_device(
    features,
    w_self,
    w_neigh,
    degrees,
    local_src,
    local_dst,
    local_tiles,
    remote_src,
    remote_part,
    remote_dst,
    remote_tiles,
    cotangent,
):
    domains = lax.axis_size("dom")
    node_rows, channels = features.shape
    block_count = node_rows // TILE
    remote_count = remote_tiles.shape[0]
    slot_count = domains * CAP
    feat_blocks = features.reshape(block_count, TILE, channels)
    targets = remote_part[:, 0]
    counter = jnp.arange(remote_count, dtype=jnp.int32)
    same_before = (targets[:, None] == targets[None, :]) & (counter[None, :] < counter[:, None])
    position = jnp.sum(jnp.where(same_before, 1, 0), axis=1).astype(jnp.int32)
    slot_index = targets * CAP + position
    local_part = local_sum(local_tiles, local_src, local_dst, feat_blocks, block_count)
    pushed = tile_products(remote_tiles, remote_src, feat_blocks).astype(jnp.bfloat16)
    outgoing = jnp.zeros((slot_count, TILE * channels), jnp.bfloat16)
    outgoing = outgoing.at[slot_index].set(pushed.reshape(remote_count, TILE * channels))
    out_blocks = jnp.zeros((slot_count,), jnp.int32).at[slot_index].set(remote_dst)
    received, got_blocks = push_partials(
        outgoing.reshape(domains, CAP * TILE * channels), out_blocks.reshape(domains, CAP)
    )
    incoming = received.reshape(slot_count, TILE * channels)
    got_index = got_blocks.reshape(slot_count)
    onehot_in = (jnp.arange(block_count, dtype=jnp.int32)[:, None] == got_index[None, :]).astype(
        jnp.bfloat16
    )
    remote_part_sum = jnp.dot(onehot_in, incoming, preferred_element_type=jnp.float32)
    summed = (local_part + remote_part_sum).reshape(node_rows, channels)
    divisor = degrees.astype(jnp.float32)[:, None]
    averaged = (summed / divisor).astype(jnp.bfloat16)
    joined = jnp.concatenate([features, averaged], axis=1)
    weights = jnp.concatenate([w_self, w_neigh], axis=0)
    partial_value = jnp.dot(joined, weights, preferred_element_type=jnp.float32)
    preact = lax.psum_scatter(
        partial_value.astype(jnp.bfloat16), "chan", scatter_dimension=1, tiled=True
    ).astype(jnp.float32)
    output = jax.nn.silu(preact).astype(jnp.bfloat16)
    slopes_own = (cotangent.astype(jnp.float32) * silu_slope(preact)).astype(jnp.bfloat16)
    slopes_all = lax.all_gather(slopes_own, "chan", axis=1, tiled=True)
    grad_terms = lax.dot_general(
        joined, slopes_all, (((0,), (0,)), ((), ())), preferred_element_type=jnp.float32
    )
    grad_sums = lax.psum(grad_terms, "dom") * (1.0 / math.sqrt(float(node_rows * domains)))
    grad_self = grad_sums[:channels]
    grad_neigh = grad_sums[channels:]
    backward = lax.dot_general(
        slopes_all, weights, (((1,), (1,)), ((), ())), preferred_element_type=jnp.float32
    )
    back_self = backward[:, :channels]
    back_rows = (backward[:, channels:] / divisor).astype(jnp.bfloat16)
    back_blocks = back_rows.reshape(block_count, TILE, channels)
    returning = jnp.take(back_blocks.reshape(block_count, TILE * channels), got_index, axis=0)
    returned = lax.all_to_all(
        returning.reshape(domains, CAP * TILE * channels),
        "dom",
        split_axis=0,
        concat_axis=0,
        tiled=True,
    )
    returned = returned.reshape(slot_count, TILE, channels)
    remote_rows = jnp.take(returned, slot_index, axis=0)
    remote_terms = jnp.einsum(
        "tij,tjc->tic", remote_tiles, remote_rows, preferred_element_type=jnp.float32
    )
    onehot_remote = (
        jnp.arange(block_count, dtype=jnp.int32)[:, None] == remote_src[None, :]
    ).astype(jnp.float32)
    remote_back = jnp.einsum(
        "bt,tk->bk",
        onehot_remote,
        remote_terms.reshape(remote_count, -1),
        precision=lax.Precision.HIGHEST,
    )
    local_rows = jnp.take(back_blocks, local_dst, axis=0)
    local_terms = jnp.einsum(
        "tij,tjc->tic", local_tiles, local_rows, preferred_element_type=jnp.float32
    )
    onehot_local = (jnp.arange(block_count, dtype=jnp.int32)[:, None] == local_src[None, :]).astype(
        jnp.float32
    )
    local_back = jnp.einsum(
        "bt,tk->bk",
        onehot_local,
        local_terms.reshape(local_terms.shape[0], -1),
        precision=lax.Precision.HIGHEST,
    )
    gathered = (remote_back + local_back).reshape(node_rows, channels)
    grad_features = (back_self + gathered).astype(jnp.bfloat16)
    return (output, grad_self, grad_neigh, grad_features)


def solution(mesh):
    in_specs = (
        P("dom", "chan"),
        P("chan", None),
        P("chan", None),
        P("dom"),
        P("dom"),
        P("dom"),
        P("dom", None, None),
        P("dom"),
        P("dom", None),
        P("dom"),
        P("dom", None, None),
        P("dom", "chan"),
    )
    out_specs = (P("dom", "chan"), P("chan", None), P("chan", None), P("dom", "chan"))
    return jax.shard_map(
        per_device, mesh=mesh, in_specs=in_specs, out_specs=out_specs, check_vma=False
    )
```

profile of v0, /device:TPU:0, one launch (start us, length us, event | category | flops | bytes accessed | tf_op | source)
XLA Modules:
  0.0 361.2 jit_solution(5732093317905515113)
XLA Ops:
  7.2 0.9 select_reduce_fusion
  8.1 0.7 and_bitcast_fusion
  8.8 0.8 scatter_custom_fusion
  9.5 0.7 all_to_all.16
  10.2 8.3 %all-to-all-start = ((s32[16,1,2]{2,1,0:T(1,128)}), s32[16,1,2]{2,1,0:T(1,128)S(1)}, u32[]{:S(2)}, u32[]{:S(2)}) async-start(s32[16,1,2]{2,1,0:T(1,128)} %bitcast.5), calls=%async_computation | async-start | bytes 16384 | tf_op jit(solution)/shard_map/all_to_all | solution.py:33
  18.6 0.7 compare_select_fusion.4
  19.2 0.7 compare_and_fusion.3
  19.9 5.9 %all-to-all-done = s32[16,1,2]{2,1,0:T(1,128)S(1)} async-done(((s32[16,1,2]{2,1,0:T(1,128)}), s32[16,1,2]{2,1,0:T(1,128)S(1)}, u32[]{:S(2)}, u32[]{:S(2)}) %all-to-all-start) | async-done | bytes 160 | tf_op jit(solution)/shard_map/all_to_all | solution.py:33
  25.9 1.7 gather_fusion
  27.6 0.6 fusion
  28.1 1.7 copy.71
  29.8 3.4 scatter_custom_fusion.1
  33.2 4.4 %all_to_all.21 = bf16[16,1,65536]{2,1,0:T(2,128)(2,1)} reshape(bf16[32,32768]{1,0:T(8,128)(2,1)S(1)} %scatter_custom_fusion.1) | data formatting | bytes 4194304 | tf_op jit(solution)/shard_map/all_to_all | solution.py:32
  38.0 12.9 %reduce.8 = bf16[16,65536]{1,0:T(8,128)(2,1)S(1)} reduce(bf16[16,1,65536]{2,1,0:T(2,128)(2,1)} %all_to_all.21, bf16[]{:T(256)} %broadcast.165), dimensions={1}, to_apply=%all_to_all.21.reduce_sub_computation | reduce | bytes 4194306 | tf_op jit(solution)/shard_map/all_to_all | solution.py:32
  51.0 2.8 reshape.226
  53.8 3.8 %all-to-all-start.1 = ((bf16[16,2,32768]{2,1,0:T(2,128)(2,1)}), bf16[16,2,32768]{2,1,0:T(2,128)(2,1)S(1)}, u32[]{:S(2)}, u32[]{:S(2)}) async-start(bf16[16,2,32768]{2,1,0:T(2,128)(2,1)} %reshape.226), calls=%async_computation.1 | async-start | bytes 4194304 | tf_op jit(solution)/shard_map/all_to_all | solution.py:32
  57.9 1.4 gather_fusion.3
  59.3 2.4 convolution_bitcast_fusion.2
  61.8 2.6 copy.54
  64.3 1.9 copy.70
  66.2 0.7 constant_dynamic-update-slice_fusion.1
  67.0 0.7 constant_dynamic-update-slice_fusion
  67.7 1.6 fusion.27
  69.2 0.5 broadcast.161
  69.8 0.7 reduce.7
  70.5 29.3 %all-to-all-done.1 = bf16[16,2,32768]{2,1,0:T(2,128)(2,1)S(1)} async-done(((bf16[16,2,32768]{2,1,0:T(2,128)(2,1)}), bf16[16,2,32768]{2,1,0:T(2,128)(2,1)S(1)}, u32[]{:S(2)}, u32[]{:S(2)}) %all-to-all-start.1) | async-done | bytes 2097184 | tf_op jit(solution)/shard_map/all_to_all | solution.py:32
  99.9 6.7 %reshape.227 = bf16[16,1,65536]{2,1,0:T(2,128)(2,1)} reshape(bf16[16,2,32768]{2,1,0:T(2,128)(2,1)S(1)} %all-to-all-done.1) | data formatting | bytes 4194304
  106.6 12.4 %reduce.1 = bf16[16,65536]{1,0:T(8,128)(2,1)S(1)} reduce(bf16[16,1,65536]{2,1,0:T(2,128)(2,1)} %reshape.227, bf16[]{:T(256)} %constant.72), dimensions={1}, to_apply=%all_to_all.19.reduce_sub_computation | reduce | bytes 4194306 | tf_op jit(solution)/shard_map/all_to_all | solution.py:32
  119.0 1.9 reshape.137
  120.8 2.2 convolution_add_fusion.1
  123.5 0.8 copy-done.8
  124.3 2.8 convolution_convert_fusion
  127.3 12.4 %reduce-scatter.2.cloned.1.call-done = bf16[1024,256]{1,0:T(8,128)(2,1)} async-done(((bf16[1024,512]{1,0:T(8,128)(2,1)}), bf16[1024,256]{1,0:T(8,128)(2,1)}) %reduce-scatter.2.cloned.1.call-update) | async-done | bytes 524304 | tf_op jit(solution)/shard_map/reduce_scatter | solution.py:82
  139.7 2.5 fusion.8
  142.4 1.2 broadcast_in_dim.80
  143.6 3.9 %broadcast_in_dim.81 = pred[16,1,65536]{2,0,1:T(8,128)(4,1)} reshape(pred[16,2,32768]{2,1,0:T(4,128)(4,1)S(1)} %broadcast_in_dim.80) | data formatting | bytes 2097152 | tf_op jit(solution)/shard_map/jit(_take)/broadcast_in_dim | solution.py:100
  147.5 4.8 %all-gather.2.cloned.1.call-done = bf16[1024,512]{1,0:T(8,128)(2,1)} async-done(((bf16[1024,256]{1,0:T(8,128)(2,1)}), bf16[1024,512]{1,0:T(8,128)(2,1)}) %all-gather.2.cloned.1.call-update) | async-done | bytes 1048592 | tf_op jit(solution)/shard_map/all_gather | solution.py:87
  152.4 2.1 fusion.43
  154.5 1.3 copy-done.1
  156.3 0.5 copy-done.5
  156.8 1.9 gather_fusion.1
  158.7 1.9 gather.19
  160.6 2.2 broadcast_select_fusion
  162.8 2.8 reduce.9
  165.6 4.0 %reshape.228 = bf16[16,2,32768]{2,1,0:T(2,128)(2,1)} reshape(bf16[16,65536]{1,0:T(8,128)(2,1)} %reduce.9) | data formatting | bytes 4194304
  169.6 7.0 %all-to-all-start.2 = ((bf16[16,2,32768]{2,1,0:T(2,128)(2,1)}), bf16[16,2,32768]{2,1,0:T(2,128)(2,1)S(1)}, u32[]{:S(2)}, u32[]{:S(2)}) async-start(bf16[16,2,32768]{2,1,0:T(2,128)(2,1)} %reshape.228), calls=%async_computation.3 | async-start | bytes 4194304 | tf_op jit(solution)/shard_map/all_to_all | solution.py:101
  176.9 3.1 fusion.17
  180.1 1.6 gather_fusion.4
  181.7 1.4 convolution_bitcast_fusion.1
  183.1 2.6 copy.65
  185.7 2.8 copy.73
  188.5 127.0 %all-reduce.2.cloned.1.call-done = f32[512,512]{1,0:T(8,128)} async-done(((f32[512,512]{1,0:T(8,128)}), f32[512,512]{1,0:T(8,128)}) %all-reduce.2.cloned.1.call-update) | async-done | bytes 1048592 | tf_op jit(solution)/shard_map/psum | solution.py:91
  315.5 1.3 broadcast_multiply_fusion
  316.9 1.0 fusion.42
  317.9 6.7 %reshape.229 = bf16[16,1,65536]{2,1,0:T(2,128)(2,1)} reshape(bf16[16,2,32768]{2,1,0:T(2,128)(2,1)S(1)} %all-to-all-done.2) | data formatting | bytes 4194304
  324.6 12.4 %reduce.3 = bf16[16,65536]{1,0:T(8,128)(2,1)S(1)} reduce(bf16[16,1,65536]{2,1,0:T(2,128)(2,1)} %reshape.229, bf16[]{:T(256)} %constant.72), dimensions={1}, to_apply=%all_to_all.20.reduce_sub_computation | reduce | bytes 4194306 | tf_op jit(solution)/shard_map/all_to_all | solution.py:101
  337.0 2.0 reshape.140
  339.0 3.2 gather_fusion.2
  342.2 1.8 convolution_bitcast_fusion
  344.0 2.0 copy.72
  346.0 2.5 fusion.28
  348.5 1.6 convolution_add_fusion
  350.2 2.3 reshape.144
  352.5 2.2 fusion.10
  (55 shorter events, 2.6 us)
Async XLA Ops:
  7.2 20.4 %copy-start = (bf16[16,128,128]{2,1,0:T(8,128)(2,1)S(1)}, bf16[16,128,128]{2,1,0:T(8,128)(2,1)}, u32[]{:S(2)}) copy-start(bf16[16,128,128]{2,1,0:T(8,128)(2,1)} %param.24) | copy-start | bytes 1572868
  10.2 15.6 %all-to-all-start = ((s32[16,1,2]{2,1,0:T(1,128)}), s32[16,1,2]{2,1,0:T(1,128)S(1)}, u32[]{:S(2)}, u32[]{:S(2)}) async-start(s32[16,1,2]{2,1,0:T(1,128)} %bitcast.5), calls=%async_computation | async-start | bytes 16384 | tf_op jit(solution)/shard_map/all_to_all | solution.py:33
  53.8 4.1 %copy-start.15 = (s32[8]{0:T(128)S(1)}, s32[8]{0:T(128)}, u32[]{:S(2)}) copy-start(s32[8]{0:T(128)} %param.18) | copy-start | bytes 100
  53.8 4.1 %copy-start.3 = (bf16[1024,256]{1,0:T(8,128)(2,1)S(1)}, bf16[1024,256]{1,0:T(8,128)(2,1)}, u32[]{:S(2)}) copy-start(bf16[1024,256]{1,0:T(8,128)(2,1)} %param.14) | copy-start | bytes 1572868
  53.8 5.5 %copy-start.7 = (bf16[8,128,128]{2,1,0:T(8,128)(2,1)S(1)}, bf16[8,128,128]{2,1,0:T(8,128)(2,1)}, u32[]{:S(2)}) copy-start(bf16[8,128,128]{2,1,0:T(8,128)(2,1)} %param.20) | copy-start | bytes 786436
  53.8 46.1 %all-to-all-start.1 = ((bf16[16,2,32768]{2,1,0:T(2,128)(2,1)}), bf16[16,2,32768]{2,1,0:T(2,128)(2,1)S(1)}, u32[]{:S(2)}, u32[]{:S(2)}) async-start(bf16[16,2,32768]{2,1,0:T(2,128)(2,1)} %reshape.226), calls=%async_computation.1 | async-start | bytes 4194304 | tf_op jit(solution)/shard_map/all_to_all | solution.py:32
  57.6 82.1 %reduce-scatter.2.cloned.1.call-start = ((), (), s32[]{:S(2)}) async-start(), calls=%async_computation.4 | async-start | bytes 1572864 | tf_op jit(solution)/shard_map/reduce_scatter | solution.py:82
  61.8 4.5 %copy-start.12 = (s32[1024]{0:T(1024)S(1)}, s32[1024]{0:T(1024)}, u32[]{:S(2)}) copy-start(s32[1024]{0:T(1024)} %param.17) | copy-start | bytes 12292
  64.3 1.9 copy-start.10
  64.3 2.7 copy-start.11
  64.3 3.4 copy-start.13
  123.5 0.8 copy-start.8
  124.3 15.5 %copy-start.9 = (bf16[1024,256]{1,0:T(8,128)(2,1)S(1)}, bf16[1024,256]{1,0:T(8,128)(2,1)}, u32[]{:S(2)}) copy-start(bf16[1024,256]{1,0:T(8,128)(2,1)} %param.25) | copy-start | bytes 1572868
  127.1 25.3 %all-gather.2.cloned.1.call-start = ((), (), s32[]{:S(2)}) async-start(), calls=%async_computation.5 | async-start | bytes 1572864 | tf_op jit(solution)/shard_map/all_gather | solution.py:87
  154.5 1.3 copy-start.1
  156.0 0.8 copy-start.5
  169.6 7.3 %copy-start.4 = (bf16[1024,256]{1,0:T(8,128)(2,1)S(1)}, bf16[1024,256]{1,0:T(8,128)(2,1)}, u32[]{:S(2)}) copy-start(bf16[1024,256]{1,0:T(8,128)(2,1)} %param.14) | copy-start | bytes 1572868
  169.6 148.3 %all-to-all-start.2 = ((bf16[16,2,32768]{2,1,0:T(2,128)(2,1)}), bf16[16,2,32768]{2,1,0:T(2,128)(2,1)S(1)}, u32[]{:S(2)}, u32[]{:S(2)}) async-start(bf16[16,2,32768]{2,1,0:T(2,128)(2,1)} %reshape.228), calls=%async_computation.3 | async-start | bytes 4194304 | tf_op jit(solution)/shard_map/all_to_all | solution.py:101
  176.6 139.0 %all-reduce.2.cloned.1.call-start = ((), (), s32[]{:S(2)}) async-start(), calls=%async_computation.6 | async-start | bytes 2097152 | tf_op jit(solution)/shard_map/psum | solution.py:91
  344.0 2.0 copy-start.14
  346.0 2.5 copy-start.6
  348.5 4.0 %copy-start.2 = (f32[1024,512]{1,0:T(8,128)S(1)}, f32[1024,512]{1,0:T(8,128)}, u32[]{:S(2)}) copy-start(f32[1024,512]{1,0:T(8,128)} %copy-done.1) | copy-start | bytes 6291460
Sparse Core Ops, SparseCore 0:
  127.2 12.4 reduce-scatter.1
  142.4 9.9 all-gather.1
  182.6 132.8 all-reduce.1
where the time goes:
time: 362 us; the launch traced here: 361 us
  waiting for transfers between devices  180 us (50%)
  local copies, waits for them, and re-layouts  72.9 us (20%)
  other arithmetic  52.6 us (15%)
  matrix products  22.1 us (6%)
  starting transfers between devices  19.9 us (5%)
  between operations  14.1 us (4%)
    psum x1, waiting for transfers between devices, per_device(): lax.psum(grad_terms, 'dom') * (1.0 / math.sqrt(float(node_rows * domains)))  127 us
    unnamed x41, local copies, waits for them, and re-layouts  32.2 us
    all_to_all x1, waiting for transfers between devices, push_partials(): lax.all_to_all(outgoing, 'dom', split_axis=0, concat_axis=0, tiled=True)  29.3 us
    all_to_all x2, other arithmetic, push_partials(): lax.all_to_all(outgoing, 'dom', split_axis=0, concat_axis=0, tiled=True)  25.3 us
    reduce_scatter x1, waiting for transfers between devices, per_device(): lax.psum_scatter(partial_value.astype(jnp.bfloat16), 'chan', scatter_dime...  12.4 us
    all_to_all x1, other arithmetic, per_device(): lax.all_to_all(returning.reshape(domains, CAP * TILE * channels), 'dom',...  12.4 us
    all_to_all x1, starting transfers between devices, push_partials(): lax.all_to_all(out_blocks, 'dom', split_axis=0, concat_axis=0, tiled=True)  8.34 us
  transfers between devices with their start and end apart: 6, of which 5 were waited for; matrix products, arithmetic and copies ran while one was open for 9% of the time, Pallas kernels for 0%

commit v1 on v0

--- a/solution.py
+++ b/solution.py
@@ -6,6 +6,12 @@
 
 TILE = 128
 CAP = 2
+
+
+def _pass_desk(z_in):
+    latest = lax.all_gather(z_in, axis_name="dom")
+    val2 = jnp.sum(latest, axis=0)
+    return val2
 
 
 def silu_slope(value):
@@ -88,7 +94,7 @@
     grad_terms = lax.dot_general(
         joined, slopes_all, (((0,), (0,)), ((), ())), preferred_element_type=jnp.float32
     )
-    grad_sums = lax.psum(grad_terms, "dom") * (1.0 / math.sqrt(float(node_rows * domains)))
+    grad_sums = _pass_desk(grad_terms) * (1.0 / math.sqrt(float(node_rows * domains)))
     grad_self = grad_sums[:channels]
     grad_neigh = grad_sums[channels:]
     backward = lax.dot_general(

time: 362 us -> 400 us (1.10)
  waiting for transfers between devices: 180 us -> 211 us
  other arithmetic: 52.6 us -> 59.5 us
    psum x1 -> x0, waiting for transfers between devices: 127 us -> none  [per_device(): lax.psum(grad_terms, 'dom') * (1.0 / math.sqrt(float(node_rows * domains)))]
    all_gather x0 -> x1, waiting for transfers between devices: none -> 97.3 us  [_pass_desk(): latest = lax.all_gather(z_in, axis_name='dom')]
    all_to_all x1, waiting for transfers between devices: 0.01 us -> 55.9 us  [per_device(): lax.all_to_all(returning.reshape(domains, CAP * TILE * channels), 'dom',...]
    reduce_sum x0 -> x1, other arithmetic: none -> 7.91 us  [_pass_desk(): val2 = jnp.sum(latest, axis=0)]
    all_gather x1, waiting for transfers between devices: 4.84 us -> 9.84 us  [per_device(): slopes_all = lax.all_gather(slopes_own, 'chan', axis=1, tiled=True)]
    unnamed x41 -> x39, local copies, waits for them, and re-layouts: 32.2 us -> 31.3 us
  transfers between devices with their start and end apart: 6 -> 6, of which waited for: 5 -> 6; matrix products, arithmetic and copies ran while one was open for 9% -> 20% of each run, Pallas kernels for 0% -> 0%
where the time goes in v1:
time: 400 us; the launch traced here: 399 us
  waiting for transfers between devices  211 us (53%)
  local copies, waits for them, and re-layouts  71.8 us (18%)
  other arithmetic  59.5 us (15%)
  matrix products  23 us (6%)
  starting transfers between devices  19.7 us (5%)
  between operations  14.1 us (4%)
    all_gather x1, waiting for transfers between devices, _pass_desk(): latest = lax.all_gather(z_in, axis_name='dom')  97.3 us
    all_to_all x1, waiting for transfers between devices, per_device(): lax.all_to_all(returning.reshape(domains, CAP * TILE * channels), 'dom',...  55.9 us
    unnamed x39, local copies, waits for them, and re-layouts  31.3 us
    all_to_all x1, waiting for transfers between devices, push_partials(): lax.all_to_all(outgoing, 'dom', split_axis=0, concat_axis=0, tiled=True)  29.3 us
    all_to_all x2, other arithmetic, push_partials(): lax.all_to_all(outgoing, 'dom', split_axis=0, concat_axis=0, tiled=True)  25.4 us
    reduce_scatter x1, waiting for transfers between devices, per_device(): lax.psum_scatter(partial_value.astype(jnp.bfloat16), 'chan', scatter_dime...  12.6 us
    all_to_all x1, other arithmetic, per_device(): lax.all_to_all(returning.reshape(domains, CAP * TILE * channels), 'dom',...  12.4 us
    all_gather x1, waiting for transfers between devices, per_device(): slopes_all = lax.all_gather(slopes_own, 'chan', axis=1, tiled=True)  9.84 us
  transfers between devices with their start and end apart: 6, of which 6 were waited for; matrix products, arithmetic and copies ran while one was open for 20% of the time, Pallas kernels for 0%

profile of v1, /device:TPU:0, one launch (start us, length us, event | category | flops | bytes accessed | tf_op | source)
XLA Modules:
  0.0 398.9 jit_solution(18375427595884846191)
XLA Ops:
  7.2 0.9 select_reduce_fusion
  8.1 0.7 and_bitcast_fusion
  8.8 0.8 scatter_custom_fusion
  9.5 0.7 all_to_all.16
  10.2 8.3 %all-to-all-start = ((s32[16,1,2]{2,1,0:T(1,128)}), s32[16,1,2]{2,1,0:T(1,128)S(1)}, u32[]{:S(2)}, u32[]{:S(2)}) async-start(s32[16,1,2]{2,1,0:T(1,128)} %bitcast.5), calls=%async_computation | async-start | bytes 16384 | tf_op jit(solution)/shard_map/all_to_all | solution.py:39
  18.6 0.7 compare_select_fusion.4
  19.2 0.7 compare_and_fusion.3
  19.9 5.9 %all-to-all-done = s32[16,1,2]{2,1,0:T(1,128)S(1)} async-done(((s32[16,1,2]{2,1,0:T(1,128)}), s32[16,1,2]{2,1,0:T(1,128)S(1)}, u32[]{:S(2)}, u32[]{:S(2)}) %all-to-all-start) | async-done | bytes 160 | tf_op jit(solution)/shard_map/all_to_all | solution.py:39
  25.9 1.7 gather_fusion
  27.6 0.6 fusion
  28.1 1.7 copy.71
  29.8 3.4 scatter_custom_fusion.1
  33.2 4.4 %all_to_all.21 = bf16[16,1,65536]{2,1,0:T(2,128)(2,1)} reshape(bf16[32,32768]{1,0:T(8,128)(2,1)S(1)} %scatter_custom_fusion.1) | data formatting | bytes 4194304 | tf_op jit(solution)/shard_map/all_to_all | solution.py:38
  37.5 0.5 broadcast.165
  38.1 13.0 %reduce.8 = bf16[16,65536]{1,0:T(8,128)(2,1)S(1)} reduce(bf16[16,1,65536]{2,1,0:T(2,128)(2,1)} %all_to_all.21, bf16[]{:T(256)} %broadcast.165), dimensions={1}, to_apply=%all_to_all.21.reduce_sub_computation | reduce | bytes 4194306 | tf_op jit(solution)/shard_map/all_to_all | solution.py:38
  51.1 2.8 reshape.227
  53.9 3.8 all-to-all-start.1
  58.0 1.4 gather_fusion.3
  59.4 2.4 convolution_bitcast_fusion.2
  61.9 2.6 copy.54
  64.4 1.9 copy.70
  66.3 0.7 constant_dynamic-update-slice_fusion.1
  67.1 0.7 constant_dynamic-update-slice_fusion
  67.8 1.6 fusion.27
  69.9 0.7 reduce.7
  70.6 29.3 %all-to-all-done.1 = bf16[16,2,32768]{2,1,0:T(2,128)(2,1)S(1)} async-done(((bf16[16,2,32768]{2,1,0:T(2,128)(2,1)}), bf16[16,2,32768]{2,1,0:T(2,128)(2,1)S(1)}, u32[]{:S(2)}, u32[]{:S(2)}) %all-to-all-start.1) | async-done | bytes 2097184 | tf_op jit(solution)/shard_map/all_to_all | solution.py:38
  100.0 6.7 %reshape.228 = bf16[16,1,65536]{2,1,0:T(2,128)(2,1)} reshape(bf16[16,2,32768]{2,1,0:T(2,128)(2,1)S(1)} %all-to-all-done.1) | data formatting | bytes 4194304
  106.6 12.4 %reduce.1 = bf16[16,65536]{1,0:T(8,128)(2,1)S(1)} reduce(bf16[16,1,65536]{2,1,0:T(2,128)(2,1)} %reshape.228, bf16[]{:T(256)} %constant.74), dimensions={1}, to_apply=%all_to_all.19.reduce_sub_computation | reduce | bytes 4194306 | tf_op jit(solution)/shard_map/all_to_all | solution.py:38
  119.0 1.9 reshape.137
  120.9 2.2 convolution_add_fusion.1
  123.5 2.8 convolution_convert_fusion
  126.4 12.6 %reduce-scatter.2.cloned.1.call-done = bf16[1024,256]{1,0:T(8,128)(2,1)} async-done(((bf16[1024,512]{1,0:T(8,128)(2,1)}), bf16[1024,256]{1,0:T(8,128)(2,1)}) %reduce-scatter.2.cloned.1.call-update) | async-done | bytes 524304 | tf_op jit(solution)/shard_map/reduce_scatter | solution.py:88
  139.0 2.5 fusion.8
  141.8 9.8 %all-gather.4.cloned.1.call-done = bf16[1024,512]{1,0:T(8,128)(2,1)} async-done(((bf16[1024,256]{1,0:T(8,128)(2,1)}), bf16[1024,512]{1,0:T(8,128)(2,1)}) %all-gather.4.cloned.1.call-update) | async-done | bytes 1048592 | tf_op jit(solution)/shard_map/all_gather | solution.py:93
  151.6 3.0 fusion.17
  154.8 1.2 broadcast_in_dim.80
  155.9 3.9 broadcast_in_dim.81
  159.9 2.1 fusion.43
  162.0 1.3 copy-done.1
  163.8 0.5 copy-done.4
  164.3 1.9 gather_fusion.1
  166.2 1.9 gather.19
  168.1 2.2 broadcast_select_fusion
  170.3 2.9 reduce.9
  173.2 4.0 %reshape.229 = bf16[16,2,32768]{2,1,0:T(2,128)(2,1)} reshape(bf16[16,65536]{1,0:T(8,128)(2,1)} %reduce.9) | data formatting | bytes 4194304
  177.2 7.0 %all-to-all-start.2 = ((bf16[16,2,32768]{2,1,0:T(2,128)(2,1)}), bf16[16,2,32768]{2,1,0:T(2,128)(2,1)S(1)}, u32[]{:S(2)}, u32[]{:S(2)}) async-start(bf16[16,2,32768]{2,1,0:T(2,128)(2,1)} %reshape.229), calls=%async_computation.3 | async-start | bytes 4194304 | tf_op jit(solution)/shard_map/all_to_all | solution.py:107
  184.2 1.4 gather_fusion.4
  185.6 2.5 convolution_bitcast_fusion.1
  188.1 2.6 copy.65
  190.6 2.8 copy.73
  193.5 55.9 %all-to-all-done.2 = bf16[16,2,32768]{2,1,0:T(2,128)(2,1)S(1)} async-done(((bf16[16,2,32768]{2,1,0:T(2,128)(2,1)}), bf16[16,2,32768]{2,1,0:T(2,128)(2,1)S(1)}, u32[]{:S(2)}, u32[]{:S(2)}) %all-to-all-start.2) | async-done | bytes 2097184 | tf_op jit(solution)/shard_map/all_to_all | solution.py:107
  249.3 6.7 %reshape.230 = bf16[16,1,65536]{2,1,0:T(2,128)(2,1)} reshape(bf16[16,2,32768]{2,1,0:T(2,128)(2,1)S(1)} %all-to-all-done.2) | data formatting | bytes 4194304
  256.0 12.4 %reduce.3 = bf16[16,65536]{1,0:T(8,128)(2,1)S(1)} reduce(bf16[16,1,65536]{2,1,0:T(2,128)(2,1)} %reshape.230, bf16[]{:T(256)} %constant.74), dimensions={1}, to_apply=%all_to_all.20.reduce_sub_computation | reduce | bytes 4194306 | tf_op jit(solution)/shard_map/all_to_all | solution.py:107
  268.4 2.0 reshape.140
  270.4 3.2 gather_fusion.2
  273.6 1.8 convolution_bitcast_fusion
  275.4 2.0 copy.72
  277.4 2.5 fusion.28
  279.9 1.6 convolution_add_fusion
  281.5 2.4 reshape.144
  283.9 2.2 fusion.10
  286.0 97.3 %all-gather.6.cloned.1.call-done = f32[8192,512]{1,0:T(8,128)} async-done(((f32[512,512]{1,0:T(8,128)}), f32[8192,512]{1,0:T(8,128)}) %all-gather.6.cloned.1.call-update) | async-done | bytes 16777232 | tf_op jit(solution)/shard_map/all_gather | solution.py:12
  383.3 7.9 %reduce_sum.22 = f32[512,512]{1,0:T(8,128)S(1)} reduce(f32[16,512,512]{2,1,0:T(8,128)} %bitcast.48, f32[]{:T(128)} %constant.51.clone.1), dimensions={0}, to_apply=%region_4.6 | reduce | flops 3932160 | bytes 17825796 | tf_op jit(solution)/shard_map/reduce_sum | solution.py:13
  391.4 1.0 fusion.42
  (54 shorter events, 2.5 us)
Async XLA Ops:
  7.2 20.4 %copy-start = (bf16[16,128,128]{2,1,0:T(8,128)(2,1)S(1)}, bf16[16,128,128]{2,1,0:T(8,128)(2,1)}, u32[]{:S(2)}) copy-start(bf16[16,128,128]{2,1,0:T(8,128)(2,1)} %param.24) | copy-start | bytes 1572868
  10.2 15.6 %all-to-all-start = ((s32[16,1,2]{2,1,0:T(1,128)}), s32[16,1,2]{2,1,0:T(1,128)S(1)}, u32[]{:S(2)}, u32[]{:S(2)}) async-start(s32[16,1,2]{2,1,0:T(1,128)} %bitcast.5), calls=%async_computation | async-start | bytes 16384 | tf_op jit(solution)/shard_map/all_to_all | solution.py:39
  53.9 4.1 %copy-start.14 = (s32[8]{0:T(128)S(1)}, s32[8]{0:T(128)}, u32[]{:S(2)}) copy-start(s32[8]{0:T(128)} %param.18) | copy-start | bytes 100
  53.9 4.1 %copy-start.3 = (bf16[1024,256]{1,0:T(8,128)(2,1)S(1)}, bf16[1024,256]{1,0:T(8,128)(2,1)}, u32[]{:S(2)}) copy-start(bf16[1024,256]{1,0:T(8,128)(2,1)} %param.14) | copy-start | bytes 1572868
  53.9 5.5 %copy-start.7 = (bf16[8,128,128]{2,1,0:T(8,128)(2,1)S(1)}, bf16[8,128,128]{2,1,0:T(8,128)(2,1)}, u32[]{:S(2)}) copy-start(bf16[8,128,128]{2,1,0:T(8,128)(2,1)} %param.20) | copy-start | bytes 786436
  53.9 46.1 %all-to-all-start.1 = ((bf16[16,2,32768]{2,1,0:T(2,128)(2,1)}), bf16[16,2,32768]{2,1,0:T(2,128)(2,1)S(1)}, u32[]{:S(2)}, u32[]{:S(2)}) async-start(bf16[16,2,32768]{2,1,0:T(2,128)(2,1)} %reshape.227), calls=%async_computation.1 | async-start | bytes 4194304 | tf_op jit(solution)/shard_map/all_to_all | solution.py:38
  57.7 81.2 %reduce-scatter.2.cloned.1.call-start = ((), (), s32[]{:S(2)}) async-start(), calls=%async_computation.4 | async-start | bytes 1572864 | tf_op jit(solution)/shard_map/reduce_scatter | solution.py:88
  61.9 4.5 %copy-start.11 = (s32[1024]{0:T(1024)S(1)}, s32[1024]{0:T(1024)}, u32[]{:S(2)}) copy-start(s32[1024]{0:T(1024)} %param.17) | copy-start | bytes 12292
  64.4 1.9 copy-start.9
  64.4 2.7 copy-start.10
  64.4 3.4 copy-start.12
  123.5 15.5 %copy-start.8 = (bf16[1024,256]{1,0:T(8,128)(2,1)S(1)}, bf16[1024,256]{1,0:T(8,128)(2,1)}, u32[]{:S(2)}) copy-start(bf16[1024,256]{1,0:T(8,128)(2,1)} %param.25) | copy-start | bytes 1572868
  126.3 25.3 %all-gather.4.cloned.1.call-start = ((), (), s32[]{:S(2)}) async-start(), calls=%async_computation.5 | async-start | bytes 1572864 | tf_op jit(solution)/shard_map/all_gather | solution.py:93
  141.5 241.8 %all-gather.6.cloned.1.call-start = ((), (), s32[]{:S(2)}) async-start(), calls=%async_computation.6 | async-start | bytes 17825792 | tf_op jit(solution)/shard_map/all_gather | solution.py:12
  162.0 1.3 copy-start.1
  163.5 0.8 copy-start.4
  177.2 7.0 %copy-start.5 = (bf16[1024,256]{1,0:T(8,128)(2,1)S(1)}, bf16[1024,256]{1,0:T(8,128)(2,1)}, u32[]{:S(2)}) copy-start(bf16[1024,256]{1,0:T(8,128)(2,1)} %copy-done.4) | copy-start | bytes 1572868
  177.2 72.1 %all-to-all-start.2 = ((bf16[16,2,32768]{2,1,0:T(2,128)(2,1)}), bf16[16,2,32768]{2,1,0:T(2,128)(2,1)S(1)}, u32[]{:S(2)}, u32[]{:S(2)}) async-start(bf16[16,2,32768]{2,1,0:T(2,128)(2,1)} %reshape.229), calls=%async_computation.3 | async-start | bytes 4194304 | tf_op jit(solution)/shard_map/all_to_all | solution.py:107
  275.4 2.0 copy-start.13
  277.4 2.5 copy-start.6
  279.9 4.0 copy-start.2
Sparse Core Ops, SparseCore 0:
  126.4 12.4 reduce-scatter.1
  141.6 9.9 all-gather.3
  154.7 228.5 all-gather.5
